TPU v7x, 512 devices: a whole 4x4x16 slice. The times are simulated.
512 devices in a mesh: blk: 16 (over z), pen: 32 (over x, y, core).
Axes of the slice: x: 4, y: 4, z: 16, core: 2. Of those that a mesh axis runs over, the one named last changes fastest.
Arguments:
- state: bfloat16 [16, 2, 32, 512, 512], P('blk', None, None, 'pen'), may hold values from -6 to 6
- inverse_x: bfloat16 [16, 2, 512, 512], P('blk')
- inverse_y: bfloat16 [16, 2, 512, 512], P('blk')
- rates: float32 [16, 3], P('blk'), may hold values from 0.05 to 0.4
- partner: int32 [16, 2], P('blk'), may hold values from 0 to 15
- face_side: int32 [16, 2], P('blk'), may hold values from 0 to 1
- orient: int32 [16, 2], P('blk'), may hold values from 0 to 1
- offset: int32 [16, 2], P('blk'), may hold values from 0 to 31
Outputs:
- relaxed: bfloat16 [16, 2, 32, 512, 512], P('blk', None, None, 'pen')
All inputs are finite; a program needn't handle non-finite values.
Results may differ from a plain program's by a relative error of at most 0.0058.
Values may be sent and summed in bfloat16 or wider, within the bound.
No kernel may reach another device: no remote copies, remote signals or barrier semaphores. Data moves between devices by JAX's collectives and lax.ppermute only.
A program may use at most 64 MiB of HBM per device.

v0:
```python
import jax
import jax.numpy as jnp
from jax import lax
from jax.sharding import PartitionSpec as P

STEPS = 2


def plane_ghosts(layers, partner_row, side_row, orient_row, offset_row, tile_rows):
    copies = jnp.broadcast_to(layers[None], (lax.axis_size("blk"),) + layers.shape)
    blocks = lax.all_to_all(copies, "blk", split_axis=0, concat_axis=0, tiled=True)
    lines = layers.shape[-1]
    rows_y = jnp.arange(lines, dtype=jnp.int32)
    result = []
    for which in range(2):
        piece = lax.dynamic_index_in_dim(blocks, partner_row[which], 0, keepdims=False)
        segment = lax.dynamic_index_in_dim(piece, side_row[which], 0, keepdims=False)
        mirrored = jnp.where(orient_row[which] == 1, lines - 1 - rows_y, rows_y)
        take_at = (mirrored + offset_row[which] * tile_rows) % lines
        result.append(jnp.take(segment, take_at, axis=-1))
    return result


def local(state, inverse_x, inverse_y, rates, partner, face_side, orient, offset):
    magnet = state[0]
    inv_x = inverse_x[0]
    inv_y = inverse_y[0]
    rate_row = rates[0]
    first_col = inv_x[:, :, 0].astype(jnp.float32)
    last_col = inv_x[:, :, -1].astype(jnp.float32)
    tile_rows = magnet.shape[2]
    planes = lax.all_to_all(magnet, "pen", split_axis=1, concat_axis=2, tiled=True)
    for repeat in range(STEPS):
        layers = jnp.stack([planes[..., 0], planes[..., -1]], axis=0)
        ghosts = plane_ghosts(layers, partner[0], face_side[0], orient[0], offset[0], tile_rows)
        interior = jnp.einsum("fax,fzyx->fzya", inv_x, planes, preferred_element_type=jnp.float32)
        edges = first_col[:, None, None, :] * ghosts[0].astype(jnp.float32)[..., None]
        edges = edges + last_col[:, None, None, :] * ghosts[1].astype(jnp.float32)[..., None]
        swept_x = (interior + edges).astype(jnp.bfloat16)
        swept_y = jnp.einsum("fcy,fzyx->fzcx", inv_y, swept_x, preferred_element_type=jnp.float32)
        proton = swept_y[0]
        carbon = swept_y[1]
        new_proton = proton - (rate_row[0] * proton + rate_row[2] * carbon)
        new_carbon = carbon - (rate_row[1] * carbon + rate_row[2] * proton)
        planes = jnp.stack([new_proton, new_carbon]).astype(jnp.bfloat16)
    magnet = lax.all_to_all(planes, "pen", split_axis=2, concat_axis=1, tiled=True)
    return magnet[None]


def solution(mesh):
    return jax.shard_map(
        local,
        mesh=mesh,
        in_specs=(
            P("blk", None, None, "pen", None),
            P("blk", None, None, None),
            P("blk", None, None, None),
            P("blk", None),
            P("blk", None),
            P("blk", None),
            P("blk", None),
            P("blk", None),
        ),
        out_specs=P("blk", None, None, "pen", None),
        check_vma=False,
    )
```

profile of v0, /device:TPU:1, one launch (start us, length us, event | category | flops | bytes accessed | tf_op | source)
XLA Modules:
  0.0 119.7 jit_solution(8040975433714026391)
XLA Ops:
  0.0 0.0 copy-start
  0.0 0.0 copy-start.8
  0.0 0.0 copy-start.9
  0.0 0.0 copy-start.2
  0.0 2.4 %copy.70 = bf16[1,2,32,16,512]{4,3,1,2,0:T(8,128)(2,1)} copy(bf16[1,2,32,16,512]{4,3,2,1,0:T(8,128)(2,1)} %param.10) | data formatting | bytes 2097152 | tf_op args[0]
  2.4 10.5 %all-to-all-start = ((bf16[2,32,16,512]{3,2,0,1:T(8,128)(2,1)}), bf16[2,32,16,512]{3,2,0,1:T(8,128)(2,1)S(1)}, u32[]{:S(2)}, u32[]{:S(2)}) async-start(bf16[2,32,16,512]{3,2,0,1:T(8,128)(2,1)} %bitcast.97), calls=%async_computation | async-start | bytes 2097152 | tf_op jit(solution)/shard_map/all_to_all | solution.py:32
  12.9 0.0 copy-done.6
  12.9 0.6 fusion.19
  16.0 0.0 copy-done.7
  16.0 0.7 fusion.18
  21.6 0.0 copy-done.8
  21.7 0.6 fusion.16
  23.4 0.7 fusion.17
  25.4 0.7 fusion.15
  26.1 3.8 %all-to-all-done = bf16[2,32,16,512]{3,2,0,1:T(8,128)(2,1)S(1)} async-done(((bf16[2,32,16,512]{3,2,0,1:T(8,128)(2,1)}), bf16[2,32,16,512]{3,2,0,1:T(8,128)(2,1)S(1)}, u32[]{:S(2)}, u32[]{:S(2)}) %all-to-all-start) | async-done | bytes 1048608 | tf_op jit(solution)/shard_map/all_to_all | solution.py:32
  29.9 0.1 copy.47
  30.0 0.3 slice_reduce_fusion.1
  30.3 0.7 broadcast_in_dim.20
  31.0 13.0 %all-to-all-start.1 = ((bf16[16,2,2,1,512]{4,2,3,1,0:T(2,128)(2,1)}), bf16[16,2,2,1,512]{4,2,3,1,0:T(2,128)(2,1)S(1)}, u32[]{:S(2)}, u32[]{:S(2)}) async-start(bf16[16,2,2,1,512]{4,2,3,1,0:T(2,128)(2,1)} %broadcast_in_dim.20), calls=%async_computation.1 | async-start | bytes 131072 | tf_op jit(solution)/shard_map/all_to_all | solution.py:11
  44.0 1.3 %convert_reduce_fusion.1 = (f32[2,512]{1,0:T(2,128)S(1)}, f32[2,512]{1,0:T(2,128)S(1)}) fusion(bf16[2,512,512]{2,1,0:T(8,128)(2,1)} %bitcast.102), kind=kLoop, calls=%fused_computation.20 | loop fusion | flops 2048 | bytes 12288 | tf_op jit(solution)/shard_map/convert_element_type | solution.py:29
  45.3 10.2 %all-to-all-done.1 = bf16[16,2,2,1,512]{4,2,3,1,0:T(2,128)(2,1)S(1)} async-done(((bf16[16,2,2,1,512]{4,2,3,1,0:T(2,128)(2,1)}), bf16[16,2,2,1,512]{4,2,3,1,0:T(2,128)(2,1)S(1)}, u32[]{:S(2)}, u32[]{:S(2)}) %all-to-all-start.1) | async-done | bytes 65568 | tf_op jit(solution)/shard_map/all_to_all | solution.py:11
  55.6 0.2 copy.49
  55.8 1.3 %gather_fusion = bf16[512,2]{1,0:T(8,128)(2,1)S(1)} fusion(bf16[2,512]{0,1:T(8,128)(2,1)S(1)} %bitcast.105, s32[1024]{0:T(1024)S(1)} %pad_clamp_fusion.1), kind=kCustom, calls=%fused_computation.clone | custom fusion | bytes 6144 | tf_op jit(solution)/shard_map/jit(_take)/gather | solution.py:20
  57.1 0.1 bitcast_convert_fusion.3
  57.3 0.1 copy.50
  57.4 0.0 copy-done.4
  57.4 0.2 copy.51
  57.6 1.3 %gather_fusion.1 = bf16[512,2]{1,0:T(8,128)(2,1)S(1)} fusion(bf16[2,512]{0,1:T(8,128)(2,1)S(1)} %bitcast.106, s32[1024]{0:T(1024)S(1)} %pad_clamp_fusion), kind=kCustom, calls=%fused_computation.1.clone | custom fusion | bytes 6144 | tf_op jit(solution)/shard_map/jit(_take)/gather | solution.py:20
  58.9 0.1 bitcast_convert_fusion.2
  59.1 0.1 copy.52
  59.2 4.0 %convolution_bitcast_fusion.1 = f32[2,1,512,512]{2,3,0,1:T(8,128)} fusion(bf16[1,2,512,512]{3,2,1,0:T(8,128)(2,1)S(1)} %copy-done, bf16[2,512,512]{2,1,0:T(8,128)(2,1)S(1)} %bitcast.99, f32[2,512]{1,0:T(2,128)S(1)} %copy.52, f32[2,512]{1,0:T(2,128)S(1)} %get-tuple-element.7, f32[2,512]{1,0:T(2,128)S(1)} %copy.50, f32[2,512]{1,0:T(2,128)S(1)} %get-tuple-element.6, ...), kind=kOutput, calls=%fused_computation.7 | convolution fusion | flops 1076363264 | bytes 5259264 | tf_op jit(solution)/shard_map/fcy,fzyx->fzcx/dot_general | solution.py:40
  63.1 3.7 %subtract_convert_fusion.3 = (bf16[1,1,512,512]{2,3,0,1:T(8,128)(2,1)S(1)}, bf16[1,1,512,512]{2,3,0,1:T(8,128)(2,1)S(1)}) fusion(f32[2,1,512,512]{2,3,0,1:T(8,128)} %convolution_bitcast_fusion.1, f32[]{:T(128)} %bitcast.27, f32[]{:T(128)} %bitcast.26, f32[]{:T(128)} %bitcast.30), kind=kLoop, calls=%fused_computation.18 | loop fusion | flops 2621440 | bytes 3145740 | tf_op jit(solution)/shard_map/convert.13
  66.9 0.0 copy-start.1
  67.0 15.5 %all_to_all.31 = bf16[16,2,2,1,512]{4,2,3,1,0:T(2,128)(2,1)S(1)} all-to-all(bf16[16,2,2,1,512]{4,2,3,1,0:T(2,128)(2,1)S(1)} %broadcast_in_dim.22), channel_id=1, replica_groups=mesh['blk'=16,'pen'=32] {'blk'}, dimensions={0} | all-to-all | bytes 131072 | tf_op jit(solution)/shard_map/all_to_all | solution.py:11
  82.5 0.2 copy.55
  82.7 1.3 %gather_fusion.2 = bf16[512,2]{1,0:T(8,128)(2,1)S(1)} fusion(bf16[2,512]{0,1:T(8,128)(2,1)S(1)} %bitcast.103, s32[1024]{0:T(1024)S(1)} %pad_clamp_fusion.1), kind=kCustom, calls=%fused_computation.2.clone | custom fusion | bytes 6144 | tf_op jit(solution)/shard_map/jit(_take)/gather | solution.py:20
  84.0 0.8 bitcast_convert_fusion.1
  84.8 0.1 copy.56
  84.9 0.2 copy.57
  85.1 1.3 %gather_fusion.3 = bf16[512,2]{1,0:T(8,128)(2,1)S(1)} fusion(bf16[2,512]{0,1:T(8,128)(2,1)S(1)} %bitcast.104, s32[1024]{0:T(1024)S(1)} %pad_clamp_fusion), kind=kCustom, calls=%fused_computation.3.clone | custom fusion | bytes 6144 | tf_op jit(solution)/shard_map/jit(_take)/gather | solution.py:20
  86.5 0.7 bitcast_convert_fusion
  87.2 0.1 copy.58
  87.3 3.9 %convolution_bitcast_fusion = f32[2,1,512,512]{2,3,0,1:T(8,128)} fusion(bf16[1,2,512,512]{3,2,1,0:T(8,128)(2,1)S(1)} %copy-done, bf16[1,512,512]{1,2,0:T(8,128)(2,1)S(1)} %bitcast.101, bf16[1,512,512]{1,2,0:T(8,128)(2,1)S(1)} %bitcast.100, f32[2,512]{1,0:T(2,128)S(1)} %copy.58, f32[2,512]{1,0:T(2,128)S(1)} %copy.56, f32[2,512]{1,0:T(2,128)} %copy-done.3, ...), kind=kOutput, calls=%fused_computation.6 | convolution fusion | flops 1076887552 | bytes 5259264 | tf_op jit(solution)/shard_map/fcy,fzyx->fzcx/dot_general | solution.py:40
  91.2 3.7 %subtract_convert_fusion.1 = (bf16[1,1,512,512]{2,3,0,1:T(8,128)(2,1)S(1)}, bf16[1,1,512,512]{2,3,0,1:T(8,128)(2,1)S(1)}) fusion(f32[2,1,512,512]{2,3,0,1:T(8,128)} %convolution_bitcast_fusion, f32[]{:T(128)} %bitcast.27, f32[]{:T(128)} %bitcast.26, f32[]{:T(128)} %bitcast.30), kind=kLoop, calls=%fused_computation.16 | loop fusion | flops 2621440 | bytes 3145740 | tf_op jit(solution)/shard_map/convert.6
  95.0 0.1 pad_maximum_fusion
  95.1 1.0 copy.60
  96.1 22.5 %all_to_all.32 = bf16[2,1,512,512]{3,0,1,2:T(2,128)(2,1)S(1)} all-to-all(bf16[2,1,512,512]{3,0,1,2:T(2,128)(2,1)S(1)} %copy.60), channel_id=1, replica_groups=mesh['blk'=16,'pen'=32] {'pen'}, dimensions={2} | all-to-all | bytes 2097152 | tf_op jit(solution)/shard_map/all_to_all | solution.py:46
  118.5 1.1 copy.61
  (24 shorter events, 0.2 us)
Async XLA Ops:
  0.0 59.2 %copy-start = (bf16[1,2,512,512]{3,2,1,0:T(8,128)(2,1)S(1)}, bf16[1,2,512,512]{3,2,1,0:T(8,128)(2,1)}, u32[]{:S(2)}) copy-start(bf16[1,2,512,512]{3,2,1,0:T(8,128)(2,1)} %param.12) | copy-start | bytes 3145732
  0.0 12.9 %copy-start.6 = (s32[1,2]{1,0:T(1,128)S(1)}, s32[1,2]{1,0:T(1,128)}, u32[]{:S(2)}) copy-start(s32[1,2]{1,0:T(1,128)} %param.14) | copy-start | bytes 28
  0.0 16.0 %copy-start.7 = (s32[1,2]{1,0:T(1,128)S(1)}, s32[1,2]{1,0:T(1,128)}, u32[]{:S(2)}) copy-start(s32[1,2]{1,0:T(1,128)} %param.15) | copy-start | bytes 28
  0.0 21.6 %copy-start.8 = (s32[1,2]{1,0:T(1,128)S(1)}, s32[1,2]{1,0:T(1,128)}, u32[]{:S(2)}) copy-start(s32[1,2]{1,0:T(1,128)} %param.16) | copy-start | bytes 28
  0.0 23.4 %copy-start.9 = (s32[1,2]{1,0:T(1,128)S(1)}, s32[1,2]{1,0:T(1,128)}, u32[]{:S(2)}) copy-start(s32[1,2]{1,0:T(1,128)} %param.17) | copy-start | bytes 28
  0.0 25.4 %copy-start.2 = (f32[1,3]{1,0:T(1,128)S(1)}, f32[1,3]{1,0:T(1,128)}, u32[]{:S(2)}) copy-start(f32[1,3]{1,0:T(1,128)} %param.13) | copy-start | bytes 40
  2.4 27.5 %all-to-all-start = ((bf16[2,32,16,512]{3,2,0,1:T(8,128)(2,1)}), bf16[2,32,16,512]{3,2,0,1:T(8,128)(2,1)S(1)}, u32[]{:S(2)}, u32[]{:S(2)}) async-start(bf16[2,32,16,512]{3,2,0,1:T(8,128)(2,1)} %bitcast.97), calls=%async_computation | async-start | bytes 2097152 | tf_op jit(solution)/shard_map/all_to_all | solution.py:32
  25.3 32.0 %copy-start.4 = (pred[512]{0:T(512)(128)(4,1)}, pred[512]{0:T(512)(128)(4,1)S(1)}, u32[]{:S(2)}) copy-start(pred[512]{0:T(512)(128)(4,1)S(1)} %compare_and_fusion.1) | copy-start | bytes 1540
  31.0 24.6 %all-to-all-start.1 = ((bf16[16,2,2,1,512]{4,2,3,1,0:T(2,128)(2,1)}), bf16[16,2,2,1,512]{4,2,3,1,0:T(2,128)(2,1)S(1)}, u32[]{:S(2)}, u32[]{:S(2)}) async-start(bf16[16,2,2,1,512]{4,2,3,1,0:T(2,128)(2,1)} %broadcast_in_dim.20), calls=%async_computation.1 | async-start | bytes 131072 | tf_op jit(solution)/shard_map/all_to_all | solution.py:11
  44.0 19.2 %copy-start.5 = (pred[512]{0:T(512)(128)(4,1)}, pred[512]{0:T(512)(128)(4,1)S(1)}, u32[]{:S(2)}) copy-start(pred[512]{0:T(512)(128)(4,1)S(1)} %compare_and_fusion) | copy-start | bytes 1540
  45.3 17.8 %copy-start.3 = (f32[2,512]{1,0:T(2,128)}, f32[2,512]{1,0:T(2,128)S(1)}, u32[]{:S(2)}) copy-start(f32[2,512]{1,0:T(2,128)S(1)} %get-tuple-element.7) | copy-start | bytes 12292
  66.9 20.4 %copy-start.1 = (bf16[1,2,512,512]{3,2,1,0:T(8,128)(2,1)S(1)}, bf16[1,2,512,512]{3,2,1,0:T(8,128)(2,1)}, u32[]{:S(2)}) copy-start(bf16[1,2,512,512]{3,2,1,0:T(8,128)(2,1)} %param.11) | copy-start | bytes 3145732
where the time goes:
time: 120 us
  blocking collectives  37.9 us (32%)
  starting transfers between devices  23.4 us (20%)
  local copies, waits for them, and re-layouts  15.3 us (13%)
  waiting for transfers between devices  14 us (12%)
  other arithmetic  10.9 us (9%)
  between operations  10.2 us (8%)
  matrix products  7.86 us (7%)
    all_to_all x1, blocking collectives, local(): lax.all_to_all(planes, 'pen', split_axis=2, concat_axis=1, tiled=True)  22.5 us
    all_to_all x1, blocking collectives, plane_ghosts(): lax.all_to_all(copies, 'blk', split_axis=0, concat_axis=0, tiled=True)  15.5 us
    all_to_all x1, starting transfers between devices, plane_ghosts(): lax.all_to_all(copies, 'blk', split_axis=0, concat_axis=0, tiled=True)  13 us
    all_to_all x1, starting transfers between devices, local(): lax.all_to_all(magnet, 'pen', split_axis=1, concat_axis=2, tiled=True)  10.5 us
    all_to_all x1, waiting for transfers between devices, plane_ghosts(): lax.all_to_all(copies, 'blk', split_axis=0, concat_axis=0, tiled=True)  10.2 us
    dot_general x2, matrix products, local(): jnp.einsum('fcy,fzyx->fzcx', inv_y, swept_x, preferred_element_type=jnp.f...  7.86 us
    another operation x2, other arithmetic  7.49 us
    gather x4, local copies, waits for them, and re-layouts, plane_ghosts(): result.append(jnp.take(segment, take_at, axis=-1))  5.36 us
  transfers between devices with their start and end apart: 2, of which 2 were waited for; matrix products, arithmetic and copies ran while one was open for 4% of the time, Pallas kernels for 0%

commit v1 on v0

--- a/solution.py
+++ b/solution.py
@@ -1,14 +1,39 @@
+import functools
 import jax
 import jax.numpy as jnp
 from jax import lax
 from jax.sharding import PartitionSpec as P
+from jax.lax import axis_index, ppermute, psum
 
 STEPS = 2
 
 
+def remake_the_ports(frame_in, ax_name):
+    front, g_now = (psum(1, ax_name), axis_index(ax_name))
+    block_out = frame_in.shape[0] // front
+    raw_out = list(frame_in.shape)
+    raw_out[0] = block_out
+    z1 = raw_out[0]
+    raw_out[0] = z1 * front
+    w1 = jnp.zeros(raw_out, frame_in.dtype)
+    for hop_no in [*range(front)]:
+        part_next = lax.dynamic_slice_in_dim(
+            frame_in, (g_now ^ hop_no) * block_out, block_out, axis=0
+        )
+        if hop_no:
+            part_next = ppermute(
+                part_next, ax_name, [(tick, tick ^ hop_no) for tick in range(front)]
+            )
+        w1 = lax.dynamic_update_slice_in_dim(w1, part_next, (g_now ^ hop_no) * z1, axis=0)
+    return w1
+
+
+do_area_here = functools.partial(remake_the_ports, ax_name="blk")
+
+
 def plane_ghosts(layers, partner_row, side_row, orient_row, offset_row, tile_rows):
     copies = jnp.broadcast_to(layers[None], (lax.axis_size("blk"),) + layers.shape)
-    blocks = lax.all_to_all(copies, "blk", split_axis=0, concat_axis=0, tiled=True)
+    blocks = do_area_here(copies)
     lines = layers.shape[-1]
     rows_y = jnp.arange(lines, dtype=jnp.int32)
     result = []

time: 120 us -> 274 us (2.28)
  starting transfers between devices: 23.4 us -> 159 us
  local copies, waits for them, and re-layouts: 15.3 us -> 52.2 us
  waiting for transfers between devices: 14 us -> 3.49 us
  blocking collectives: 37.9 us -> 28.6 us
    ppermute x0 -> x30, starting transfers between devices: none -> 149 us  [remake_the_ports(): ppermute(part_next, ax_name, [(tick, tick ^ hop_no) for tick in range(fro...]
    dynamic_update_slice x0 -> x32, local copies, waits for them, and re-layouts: none -> 23.3 us  [remake_the_ports(): lax.dynamic_update_slice_in_dim(w1, part_next, (g_now ^ hop_no) * z1, axi...]
    all_to_all x1 -> x0, blocking collectives: 15.5 us -> none  [plane_ghosts(): lax.all_to_all(copies, 'blk', split_axis=0, concat_axis=0, tiled=True)]
    all_to_all x1 -> x0, starting transfers between devices: 13 us -> none  [plane_ghosts(): lax.all_to_all(copies, 'blk', split_axis=0, concat_axis=0, tiled=True)]
    all_to_all x1 -> x0, waiting for transfers between devices: 10.2 us -> none  [plane_ghosts(): lax.all_to_all(copies, 'blk', split_axis=0, concat_axis=0, tiled=True)]
    another operation x0 -> x4, local copies, waits for them, and re-layouts: none -> 7.82 us
    ppermute x0 -> x30, local copies, waits for them, and re-layouts: none -> 6.26 us  [remake_the_ports(): ppermute(part_next, ax_name, [(tick, tick ^ hop_no) for tick in range(fro...]
    all_to_all x1, blocking collectives: 22.5 us -> 28.6 us  [local(): lax.all_to_all(planes, 'pen', split_axis=2, concat_axis=1, tiled=True)]
  transfers between devices with their start and end apart: 2 -> 31, of which waited for: 2 -> 1; matrix products, arithmetic and copies ran while one was open for 4% -> 14% of each run, Pallas kernels for 0% -> 0%
where the time goes in v1:
time: 274 us; the launch traced here: 271 us
  starting transfers between devices  159 us (58%)
  local copies, waits for them, and re-layouts  52.2 us (19%)
  blocking collectives  28.6 us (10%)
  between operations  10.7 us (4%)
  other arithmetic  9.6 us (4%)
  matrix products  7.79 us (3%)
  waiting for transfers between devices  3.49 us (1%)
    ppermute x30, starting transfers between devices, remake_the_ports(): ppermute(part_next, ax_name, [(tick, tick ^ hop_no) for tick in range(fro...  149 us
    all_to_all x1, blocking collectives, local(): lax.all_to_all(planes, 'pen', split_axis=2, concat_axis=1, tiled=True)  28.6 us
    dynamic_update_slice x32, local copies, waits for them, and re-layouts, remake_the_ports(): lax.dynamic_update_slice_in_dim(w1, part_next, (g_now ^ hop_no) * z1, axi...  23.3 us
    all_to_all x1, starting transfers between devices, local(): lax.all_to_all(magnet, 'pen', split_axis=1, concat_axis=2, tiled=True)  10.5 us
    dot_general x2, matrix products, local(): jnp.einsum('fcy,fzyx->fzcx', inv_y, swept_x, preferred_element_type=jnp.f...  7.79 us
    another operation x2, other arithmetic  7.65 us
    ppermute x30, local copies, waits for them, and re-layouts, remake_the_ports(): ppermute(part_next, ax_name, [(tick, tick ^ hop_no) for tick in range(fro...  6.26 us
    gather x4, local copies, waits for them, and re-layouts, plane_ghosts(): result.append(jnp.take(segment, take_at, axis=-1))  5.95 us
  transfers between devices with their start and end apart: 31, of which 1 were waited for; matrix products, arithmetic and copies ran while one was open for 14% of the time, Pallas kernels for 0%

profile of v1, /device:TPU:1, one launch (start us, length us, event | category | flops | bytes accessed | tf_op | source)
XLA Modules:
  0.0 271.4 jit_solution(13799913106358223308)
XLA Ops:
  0.1 2.4 copy.197
  2.5 10.5 %all-to-all-start = ((bf16[2,32,16,512]{3,2,0,1:T(8,128)(2,1)}), bf16[2,32,16,512]{3,2,0,1:T(8,128)(2,1)S(1)}, u32[]{:S(2)}, u32[]{:S(2)}) async-start(bf16[2,32,16,512]{3,2,0,1:T(8,128)(2,1)} %bitcast.101), calls=%async_computation | async-start | bytes 2097152 | tf_op jit(solution)/shard_map/all_to_all | solution.py:57
  26.5 3.4 %all-to-all-done = bf16[2,32,16,512]{3,2,0,1:T(8,128)(2,1)S(1)} async-done(((bf16[2,32,16,512]{3,2,0,1:T(8,128)(2,1)}), bf16[2,32,16,512]{3,2,0,1:T(8,128)(2,1)S(1)}, u32[]{:S(2)}, u32[]{:S(2)}) %all-to-all-start) | async-done | bytes 1048608 | tf_op jit(solution)/shard_map/all_to_all | solution.py:57
  30.6 1.9 collective-permute-start
  32.5 4.6 %collective-permute-start.1 = (bf16[1,2,2,1,512]{4,2,1,3,0:T(2,128)(2,1)S(1)}, bf16[1,2,2,1,512]{4,2,1,3,0:T(2,128)(2,1)S(1)}, u32[]{:S(2)}, u32[]{:S(2)}) collective-permute-start(bf16[1,2,2,1,512]{4,2,1,3,0:T(2,128)(2,1)S(1)} %maximum_bitcast_fusion), channel_id=1, source_target_pairs={{0,64},{32,96},{64,0},{96,32},{128,192},{160,224},{192,128},{224,1... | collective-permute-start | bytes 12296 | tf_op jit(solution)/shard_map/ppermute | solution.py:24
  37.1 2.8 %collective-permute-start.2 = (bf16[1,2,2,1,512]{4,2,1,3,0:T(2,128)(2,1)S(1)}, bf16[1,2,2,1,512]{4,2,1,3,0:T(2,128)(2,1)S(1)}, u32[]{:S(2)}, u32[]{:S(2)}) collective-permute-start(bf16[1,2,2,1,512]{4,2,1,3,0:T(2,128)(2,1)S(1)} %maximum_bitcast_fusion), channel_id=1, source_target_pairs={{0,96},{32,64},{64,32},{96,0},{128,224},{160,192},{192,160},{224,1... | collective-permute-start | bytes 12296 | tf_op jit(solution)/shard_map/ppermute | solution.py:24
  39.9 8.0 %collective-permute-start.3 = (bf16[1,2,2,1,512]{4,2,1,3,0:T(2,128)(2,1)S(1)}, bf16[1,2,2,1,512]{4,2,1,3,0:T(2,128)(2,1)S(1)}, u32[]{:S(2)}, u32[]{:S(2)}) collective-permute-start(bf16[1,2,2,1,512]{4,2,1,3,0:T(2,128)(2,1)S(1)} %maximum_bitcast_fusion), channel_id=1, source_target_pairs={{0,128},{32,160},{64,192},{96,224},{128,0},{160,32},{192,64},{224,... | collective-permute-start | bytes 12296 | tf_op jit(solution)/shard_map/ppermute | solution.py:24
  47.8 1.9 collective-permute-start.4
  49.8 2.9 %broadcast.115.clone = bf16[16,2,2,1,512]{2,4,3,1,0:T(8,128)(2,1)} broadcast(bf16[]{:T(256)} %constant.176.clone.1), dimensions={} | broadcast | bytes 65538 | tf_op jit(solution)/shard_map/broadcast.5
  53.4 9.3 %collective-permute-start.5 = (bf16[1,2,2,1,512]{4,2,1,3,0:T(2,128)(2,1)S(1)}, bf16[1,2,2,1,512]{4,2,1,3,0:T(2,128)(2,1)S(1)}, u32[]{:S(2)}, u32[]{:S(2)}) collective-permute-start(bf16[1,2,2,1,512]{4,2,1,3,0:T(2,128)(2,1)S(1)} %maximum_bitcast_fusion), channel_id=1, source_target_pairs={{0,192},{32,224},{64,128},{96,160},{128,64},{160,96},{192,0},{224,... | collective-permute-start | bytes 12296 | tf_op jit(solution)/shard_map/ppermute | solution.py:24
  63.7 1.9 collective-permute-start.6
  66.5 12.6 %collective-permute-start.7 = (bf16[1,2,2,1,512]{4,2,1,3,0:T(2,128)(2,1)S(1)}, bf16[1,2,2,1,512]{4,2,1,3,0:T(2,128)(2,1)S(1)}, u32[]{:S(2)}, u32[]{:S(2)}) collective-permute-start(bf16[1,2,2,1,512]{4,2,1,3,0:T(2,128)(2,1)S(1)} %maximum_bitcast_fusion), channel_id=1, source_target_pairs={{0,256},{32,288},{64,320},{96,352},{128,384},{160,416},{192,448},{... | collective-permute-start | bytes 12296 | tf_op jit(solution)/shard_map/ppermute | solution.py:24
  80.0 1.9 collective-permute-start.8
  82.9 7.1 %collective-permute-start.9 = (bf16[1,2,2,1,512]{4,2,1,3,0:T(2,128)(2,1)S(1)}, bf16[1,2,2,1,512]{4,2,1,3,0:T(2,128)(2,1)S(1)}, u32[]{:S(2)}, u32[]{:S(2)}) collective-permute-start(bf16[1,2,2,1,512]{4,2,1,3,0:T(2,128)(2,1)S(1)} %maximum_bitcast_fusion), channel_id=1, source_target_pairs={{0,320},{32,352},{64,256},{96,288},{128,448},{160,480},{192,384},{... | collective-permute-start | bytes 12296 | tf_op jit(solution)/shard_map/ppermute | solution.py:24
  91.0 4.2 %collective-permute-start.10 = (bf16[1,2,2,1,512]{4,2,1,3,0:T(2,128)(2,1)S(1)}, bf16[1,2,2,1,512]{4,2,1,3,0:T(2,128)(2,1)S(1)}, u32[]{:S(2)}, u32[]{:S(2)}) collective-permute-start(bf16[1,2,2,1,512]{4,2,1,3,0:T(2,128)(2,1)S(1)} %maximum_bitcast_fusion), channel_id=1, source_target_pairs={{0,352},{32,320},{64,288},{96,256},{128,480},{160,448},{192,416},{... | collective-permute-start | bytes 12296 | tf_op jit(solution)/shard_map/ppermute | solution.py:24
  96.1 5.4 %collective-permute-start.11 = (bf16[1,2,2,1,512]{4,2,1,3,0:T(2,128)(2,1)S(1)}, bf16[1,2,2,1,512]{4,2,1,3,0:T(2,128)(2,1)S(1)}, u32[]{:S(2)}, u32[]{:S(2)}) collective-permute-start(bf16[1,2,2,1,512]{4,2,1,3,0:T(2,128)(2,1)S(1)} %maximum_bitcast_fusion), channel_id=1, source_target_pairs={{0,384},{32,416},{64,448},{96,480},{128,256},{160,288},{192,320},{... | collective-permute-start | bytes 12296 | tf_op jit(solution)/shard_map/ppermute | solution.py:24
  102.5 4.6 %collective-permute-start.12 = (bf16[1,2,2,1,512]{4,2,1,3,0:T(2,128)(2,1)S(1)}, bf16[1,2,2,1,512]{4,2,1,3,0:T(2,128)(2,1)S(1)}, u32[]{:S(2)}, u32[]{:S(2)}) collective-permute-start(bf16[1,2,2,1,512]{4,2,1,3,0:T(2,128)(2,1)S(1)} %maximum_bitcast_fusion), channel_id=1, source_target_pairs={{0,416},{32,384},{64,480},{96,448},{128,288},{160,256},{192,352},{... | collective-permute-start | bytes 12296 | tf_op jit(solution)/shard_map/ppermute | solution.py:24
  108.0 7.7 %collective-permute-start.13 = (bf16[1,2,2,1,512]{4,2,1,3,0:T(2,128)(2,1)S(1)}, bf16[1,2,2,1,512]{4,2,1,3,0:T(2,128)(2,1)S(1)}, u32[]{:S(2)}, u32[]{:S(2)}) collective-permute-start(bf16[1,2,2,1,512]{4,2,1,3,0:T(2,128)(2,1)S(1)} %maximum_bitcast_fusion), channel_id=1, source_target_pairs={{0,448},{32,480},{64,384},{96,416},{128,320},{160,352},{192,256},{... | collective-permute-start | bytes 12296 | tf_op jit(solution)/shard_map/ppermute | solution.py:24
  116.7 1.9 collective-permute-start.14
  124.3 1.0 dynamic-slice_bitcast_fusion.3
  125.3 1.3 gather_fusion
  126.9 1.3 gather_fusion.1
  128.5 3.9 %convolution_bitcast_fusion.1 = f32[2,1,512,512]{2,3,0,1:T(8,128)} fusion(bf16[1,2,512,512]{3,2,1,0:T(8,128)(2,1)S(1)} %copy-done, bf16[2,512,512]{2,1,0:T(8,128)(2,1)S(1)} %bitcast.105, f32[2,512]{1,0:T(2,128)S(1)} %copy.165, f32[2,512]{1,0:T(2,128)S(1)} %get-tuple-element.7, f32[2,512]{1,0:T(2,128)S(1)} %copy.164, f32[2,512]{1,0:T(2,128)S(1)} %get-tuple-element.6, ...), kind=kOutput, calls=%fused_computation.7 | convolution fusion | flops 1076363264 | bytes 5259264 | tf_op jit(solution)/shard_map/fcy,fzyx->fzcx/dot_general | solution.py:65
  132.5 3.8 %subtract_convert_fusion.3 = (bf16[1,1,512,512]{2,3,0,1:T(8,128)(2,1)S(1)}, bf16[1,1,512,512]{2,3,0,1:T(8,128)(2,1)S(1)}) fusion(f32[2,1,512,512]{2,3,0,1:T(8,128)} %convolution_bitcast_fusion.1, f32[]{:T(128)} %bitcast.27, f32[]{:T(128)} %bitcast.26, f32[]{:T(128)} %bitcast.30), kind=kLoop, calls=%fused_computation.18 | loop fusion | flops 2621440 | bytes 3145740 | tf_op jit(solution)/shard_map/convert.13
  136.6 3.1 %collective-permute-start.15 = (bf16[1,2,2,1,512]{4,2,1,3,0:T(2,128)(2,1)S(1)}, bf16[1,2,2,1,512]{4,2,1,3,0:T(2,128)(2,1)S(1)}, u32[]{:S(2)}, u32[]{:S(2)}) collective-permute-start(bf16[1,2,2,1,512]{4,2,1,3,0:T(2,128)(2,1)S(1)} %maximum_bitcast_fusion.1), channel_id=1, source_target_pairs={{0,32},{32,0},{64,96},{96,64},{128,160},{160,128},{192,224},{224,1... | collective-permute-start | bytes 12296 | tf_op jit(solution)/shard_map/ppermute | solution.py:24
  139.6 5.4 %collective-permute-start.16 = (bf16[1,2,2,1,512]{4,2,1,3,0:T(2,128)(2,1)S(1)}, bf16[1,2,2,1,512]{4,2,1,3,0:T(2,128)(2,1)S(1)}, u32[]{:S(2)}, u32[]{:S(2)}) collective-permute-start(bf16[1,2,2,1,512]{4,2,1,3,0:T(2,128)(2,1)S(1)} %maximum_bitcast_fusion.1), channel_id=1, source_target_pairs={{0,64},{32,96},{64,0},{96,32},{128,192},{160,224},{192,128},{224,1... | collective-permute-start | bytes 12296 | tf_op jit(solution)/shard_map/ppermute | solution.py:24
  145.1 1.9 collective-permute-start.17
  147.0 6.8 %collective-permute-start.18 = (bf16[1,2,2,1,512]{4,2,1,3,0:T(2,128)(2,1)S(1)}, bf16[1,2,2,1,512]{4,2,1,3,0:T(2,128)(2,1)S(1)}, u32[]{:S(2)}, u32[]{:S(2)}) collective-permute-start(bf16[1,2,2,1,512]{4,2,1,3,0:T(2,128)(2,1)S(1)} %maximum_bitcast_fusion.1), channel_id=1, source_target_pairs={{0,128},{32,160},{64,192},{96,224},{128,0},{160,32},{192,64},{224,... | collective-permute-start | bytes 12296 | tf_op jit(solution)/shard_map/ppermute | solution.py:24
  153.8 2.4 collective-permute-start.19
  156.2 2.9 %broadcast.115 = bf16[16,2,2,1,512]{2,4,3,1,0:T(8,128)(2,1)} broadcast(bf16[]{:T(256)} %constant.176.clone.1), dimensions={} | broadcast | bytes 65538 | tf_op jit(solution)/shard_map/broadcast.5
  159.8 5.6 %collective-permute-start.20 = (bf16[1,2,2,1,512]{4,2,1,3,0:T(2,128)(2,1)S(1)}, bf16[1,2,2,1,512]{4,2,1,3,0:T(2,128)(2,1)S(1)}, u32[]{:S(2)}, u32[]{:S(2)}) collective-permute-start(bf16[1,2,2,1,512]{4,2,1,3,0:T(2,128)(2,1)S(1)} %maximum_bitcast_fusion.1), channel_id=1, source_target_pairs={{0,192},{32,224},{64,128},{96,160},{128,64},{160,96},{192,0},{224,... | collective-permute-start | bytes 12296 | tf_op jit(solution)/shard_map/ppermute | solution.py:24
  166.4 5.4 %collective-permute-start.21 = (bf16[1,2,2,1,512]{4,2,1,3,0:T(2,128)(2,1)S(1)}, bf16[1,2,2,1,512]{4,2,1,3,0:T(2,128)(2,1)S(1)}, u32[]{:S(2)}, u32[]{:S(2)}) collective-permute-start(bf16[1,2,2,1,512]{4,2,1,3,0:T(2,128)(2,1)S(1)} %maximum_bitcast_fusion.1), channel_id=1, source_target_pairs={{0,224},{32,192},{64,160},{96,128},{128,96},{160,64},{192,32},{224... | collective-permute-start | bytes 12296 | tf_op jit(solution)/shard_map/ppermute | solution.py:24
  172.7 7.8 %collective-permute-start.22 = (bf16[1,2,2,1,512]{4,2,1,3,0:T(2,128)(2,1)S(1)}, bf16[1,2,2,1,512]{4,2,1,3,0:T(2,128)(2,1)S(1)}, u32[]{:S(2)}, u32[]{:S(2)}) collective-permute-start(bf16[1,2,2,1,512]{4,2,1,3,0:T(2,128)(2,1)S(1)} %maximum_bitcast_fusion.1), channel_id=1, source_target_pairs={{0,256},{32,288},{64,320},{96,352},{128,384},{160,416},{192,448},{... | collective-permute-start | bytes 12296 | tf_op jit(solution)/shard_map/ppermute | solution.py:24
  181.4 5.3 %collective-permute-start.23 = (bf16[1,2,2,1,512]{4,2,1,3,0:T(2,128)(2,1)S(1)}, bf16[1,2,2,1,512]{4,2,1,3,0:T(2,128)(2,1)S(1)}, u32[]{:S(2)}, u32[]{:S(2)}) collective-permute-start(bf16[1,2,2,1,512]{4,2,1,3,0:T(2,128)(2,1)S(1)} %maximum_bitcast_fusion.1), channel_id=1, source_target_pairs={{0,288},{32,256},{64,352},{96,320},{128,416},{160,384},{192,480},{... | collective-permute-start | bytes 12296 | tf_op jit(solution)/shard_map/ppermute | solution.py:24
  187.7 5.4 %collective-permute-start.24 = (bf16[1,2,2,1,512]{4,2,1,3,0:T(2,128)(2,1)S(1)}, bf16[1,2,2,1,512]{4,2,1,3,0:T(2,128)(2,1)S(1)}, u32[]{:S(2)}, u32[]{:S(2)}) collective-permute-start(bf16[1,2,2,1,512]{4,2,1,3,0:T(2,128)(2,1)S(1)} %maximum_bitcast_fusion.1), channel_id=1, source_target_pairs={{0,320},{32,352},{64,256},{96,288},{128,448},{160,480},{192,384},{... | collective-permute-start | bytes 12296 | tf_op jit(solution)/shard_map/ppermute | solution.py:24
  194.0 6.8 %collective-permute-start.25 = (bf16[1,2,2,1,512]{4,2,1,3,0:T(2,128)(2,1)S(1)}, bf16[1,2,2,1,512]{4,2,1,3,0:T(2,128)(2,1)S(1)}, u32[]{:S(2)}, u32[]{:S(2)}) collective-permute-start(bf16[1,2,2,1,512]{4,2,1,3,0:T(2,128)(2,1)S(1)} %maximum_bitcast_fusion.1), channel_id=1, source_target_pairs={{0,352},{32,320},{64,288},{96,256},{128,480},{160,448},{192,416},{... | collective-permute-start | bytes 12296 | tf_op jit(solution)/shard_map/ppermute | solution.py:24
  201.8 2.9 %collective-permute-start.26 = (bf16[1,2,2,1,512]{4,2,1,3,0:T(2,128)(2,1)S(1)}, bf16[1,2,2,1,512]{4,2,1,3,0:T(2,128)(2,1)S(1)}, u32[]{:S(2)}, u32[]{:S(2)}) collective-permute-start(bf16[1,2,2,1,512]{4,2,1,3,0:T(2,128)(2,1)S(1)} %maximum_bitcast_fusion.1), channel_id=1, source_target_pairs={{0,384},{32,416},{64,448},{96,480},{128,256},{160,288},{192,320},{... | collective-permute-start | bytes 12296 | tf_op jit(solution)/shard_map/ppermute | solution.py:24
  205.6 6.4 %collective-permute-start.27 = (bf16[1,2,2,1,512]{4,2,1,3,0:T(2,128)(2,1)S(1)}, bf16[1,2,2,1,512]{4,2,1,3,0:T(2,128)(2,1)S(1)}, u32[]{:S(2)}, u32[]{:S(2)}) collective-permute-start(bf16[1,2,2,1,512]{4,2,1,3,0:T(2,128)(2,1)S(1)} %maximum_bitcast_fusion.1), channel_id=1, source_target_pairs={{0,416},{32,384},{64,480},{96,448},{128,288},{160,256},{192,352},{... | collective-permute-start | bytes 12296 | tf_op jit(solution)/shard_map/ppermute | solution.py:24
  212.9 4.4 %collective-permute-start.28 = (bf16[1,2,2,1,512]{4,2,1,3,0:T(2,128)(2,1)S(1)}, bf16[1,2,2,1,512]{4,2,1,3,0:T(2,128)(2,1)S(1)}, u32[]{:S(2)}, u32[]{:S(2)}) collective-permute-start(bf16[1,2,2,1,512]{4,2,1,3,0:T(2,128)(2,1)S(1)} %maximum_bitcast_fusion.1), channel_id=1, source_target_pairs={{0,448},{32,480},{64,384},{96,416},{128,320},{160,352},{192,256},{... | collective-permute-start | bytes 12296 | tf_op jit(solution)/shard_map/ppermute | solution.py:24
  218.3 3.2 %collective-permute-start.29 = (bf16[1,2,2,1,512]{4,2,1,3,0:T(2,128)(2,1)S(1)}, bf16[1,2,2,1,512]{4,2,1,3,0:T(2,128)(2,1)S(1)}, u32[]{:S(2)}, u32[]{:S(2)}) collective-permute-start(bf16[1,2,2,1,512]{4,2,1,3,0:T(2,128)(2,1)S(1)} %maximum_bitcast_fusion.1), channel_id=1, source_target_pairs={{0,480},{32,448},{64,416},{96,384},{128,352},{160,320},{192,288},{... | collective-permute-start | bytes 12296 | tf_op jit(solution)/shard_map/ppermute | solution.py:24
  227.2 1.0 dynamic-slice_bitcast_fusion.1
  228.2 1.9 gather_fusion.2
  230.1 1.0 bitcast_convert_fusion.1
  231.2 1.3 gather_fusion.3
  232.8 3.9 %convolution_bitcast_fusion = f32[2,1,512,512]{2,3,0,1:T(8,128)} fusion(bf16[1,2,512,512]{3,2,1,0:T(8,128)(2,1)S(1)} %copy-done, bf16[1,512,512]{1,2,0:T(8,128)(2,1)S(1)} %bitcast.107, bf16[1,512,512]{1,2,0:T(8,128)(2,1)S(1)} %bitcast.106, f32[2,512]{1,0:T(2,128)S(1)} %copy.185, f32[2,512]{1,0:T(2,128)S(1)} %copy.184, f32[2,512]{1,0:T(2,128)} %copy-done.4, ...), kind=kOutput, calls=%fused_computation.6 | convolution fusion | flops 1076887552 | bytes 5259264 | tf_op jit(solution)/shard_map/fcy,fzyx->fzcx/dot_general | solution.py:65
  236.7 3.8 %subtract_convert_fusion.1 = (bf16[1,1,512,512]{2,3,0,1:T(8,128)(2,1)S(1)}, bf16[1,1,512,512]{2,3,0,1:T(8,128)(2,1)S(1)}) fusion(f32[2,1,512,512]{2,3,0,1:T(8,128)} %convolution_bitcast_fusion, f32[]{:T(128)} %bitcast.27, f32[]{:T(128)} %bitcast.26, f32[]{:T(128)} %bitcast.30), kind=kLoop, calls=%fused_computation.16 | loop fusion | flops 2621440 | bytes 3145740 | tf_op jit(solution)/shard_map/convert.6
  241.6 28.6 %all_to_all.21 = bf16[2,1,512,512]{3,0,1,2:T(2,128)(2,1)S(1)} all-to-all(bf16[2,1,512,512]{3,0,1,2:T(2,128)(2,1)S(1)} %copy.187), channel_id=1, replica_groups=mesh['blk'=16,'pen'=32] {'pen'}, dimensions={2} | all-to-all | bytes 2097152 | tf_op jit(solution)/shard_map/all_to_all | solution.py:71
  270.3 1.1 copy.188
  (138 shorter events, 35.9 us)
Async XLA Ops:
  0.0 128.5 %copy-start = (bf16[1,2,512,512]{3,2,1,0:T(8,128)(2,1)S(1)}, bf16[1,2,512,512]{3,2,1,0:T(8,128)(2,1)}, u32[]{:S(2)}) copy-start(bf16[1,2,512,512]{3,2,1,0:T(8,128)(2,1)} %param.12) | copy-start | bytes 3145732
  0.0 13.0 %copy-start.5 = (s32[1,2]{1,0:T(1,128)S(1)}, s32[1,2]{1,0:T(1,128)}, u32[]{:S(2)}) copy-start(s32[1,2]{1,0:T(1,128)} %param.14) | copy-start | bytes 28
  0.0 14.9 %copy-start.6 = (s32[1,2]{1,0:T(1,128)S(1)}, s32[1,2]{1,0:T(1,128)}, u32[]{:S(2)}) copy-start(s32[1,2]{1,0:T(1,128)} %param.15) | copy-start | bytes 28
  0.0 21.7 %copy-start.7 = (s32[1,2]{1,0:T(1,128)S(1)}, s32[1,2]{1,0:T(1,128)}, u32[]{:S(2)}) copy-start(s32[1,2]{1,0:T(1,128)} %param.16) | copy-start | bytes 28
  0.0 23.6 %copy-start.8 = (s32[1,2]{1,0:T(1,128)S(1)}, s32[1,2]{1,0:T(1,128)}, u32[]{:S(2)}) copy-start(s32[1,2]{1,0:T(1,128)} %param.17) | copy-start | bytes 28
  0.0 25.5 %copy-start.3 = (f32[1,3]{1,0:T(1,128)S(1)}, f32[1,3]{1,0:T(1,128)}, u32[]{:S(2)}) copy-start(f32[1,3]{1,0:T(1,128)} %param.13) | copy-start | bytes 40
  0.0 26.2 %copy-start.1 = (bf16[1,2,512,512]{3,2,1,0:T(8,128)(2,1)S(1)}, bf16[1,2,512,512]{3,2,1,0:T(8,128)(2,1)}, u32[]{:S(2)}) copy-start(bf16[1,2,512,512]{3,2,1,0:T(8,128)(2,1)} %param.11) | copy-start | bytes 3145732
  2.5 27.5 %all-to-all-start = ((bf16[2,32,16,512]{3,2,0,1:T(8,128)(2,1)}), bf16[2,32,16,512]{3,2,0,1:T(8,128)(2,1)S(1)}, u32[]{:S(2)}, u32[]{:S(2)}) async-start(bf16[2,32,16,512]{3,2,0,1:T(8,128)(2,1)} %bitcast.101), calls=%async_computation | async-start | bytes 2097152 | tf_op jit(solution)/shard_map/all_to_all | solution.py:57
  26.5 102.0 %copy-start.4 = (f32[2,512]{1,0:T(2,128)}, f32[2,512]{1,0:T(2,128)S(1)}, u32[]{:S(2)}) copy-start(f32[2,512]{1,0:T(2,128)S(1)} %get-tuple-element.7) | copy-start | bytes 12292
  30.6 22.8 %collective-permute-start = (bf16[1,2,2,1,512]{4,2,1,3,0:T(2,128)(2,1)S(1)}, bf16[1,2,2,1,512]{4,2,1,3,0:T(2,128)(2,1)S(1)}, u32[]{:S(2)}, u32[]{:S(2)}) collective-permute-start(bf16[1,2,2,1,512]{4,2,1,3,0:T(2,128)(2,1)S(1)} %maximum_bitcast_fusion), channel_id=1, source_target_pairs={{0,32},{32,0},{64,96},{96,64},{128,160},{160,128},{192,224},{224,1... | collective-permute-start | bytes 12296 | tf_op jit(solution)/shard_map/ppermute | solution.py:24
  32.5 31.2 %collective-permute-start.1 = (bf16[1,2,2,1,512]{4,2,1,3,0:T(2,128)(2,1)S(1)}, bf16[1,2,2,1,512]{4,2,1,3,0:T(2,128)(2,1)S(1)}, u32[]{:S(2)}, u32[]{:S(2)}) collective-permute-start(bf16[1,2,2,1,512]{4,2,1,3,0:T(2,128)(2,1)S(1)} %maximum_bitcast_fusion), channel_id=1, source_target_pairs={{0,64},{32,96},{64,0},{96,32},{128,192},{160,224},{192,128},{224,1... | collective-permute-start | bytes 12296 | tf_op jit(solution)/shard_map/ppermute | solution.py:24
  37.1 29.5 %collective-permute-start.2 = (bf16[1,2,2,1,512]{4,2,1,3,0:T(2,128)(2,1)S(1)}, bf16[1,2,2,1,512]{4,2,1,3,0:T(2,128)(2,1)S(1)}, u32[]{:S(2)}, u32[]{:S(2)}) collective-permute-start(bf16[1,2,2,1,512]{4,2,1,3,0:T(2,128)(2,1)S(1)} %maximum_bitcast_fusion), channel_id=1, source_target_pairs={{0,96},{32,64},{64,32},{96,0},{128,224},{160,192},{192,160},{224,1... | collective-permute-start | bytes 12296 | tf_op jit(solution)/shard_map/ppermute | solution.py:24
  39.9 40.2 %collective-permute-start.3 = (bf16[1,2,2,1,512]{4,2,1,3,0:T(2,128)(2,1)S(1)}, bf16[1,2,2,1,512]{4,2,1,3,0:T(2,128)(2,1)S(1)}, u32[]{:S(2)}, u32[]{:S(2)}) collective-permute-start(bf16[1,2,2,1,512]{4,2,1,3,0:T(2,128)(2,1)S(1)} %maximum_bitcast_fusion), channel_id=1, source_target_pairs={{0,128},{32,160},{64,192},{96,224},{128,0},{160,32},{192,64},{224,... | collective-permute-start | bytes 12296 | tf_op jit(solution)/shard_map/ppermute | solution.py:24
  47.8 35.1 %collective-permute-start.4 = (bf16[1,2,2,1,512]{4,2,1,3,0:T(2,128)(2,1)S(1)}, bf16[1,2,2,1,512]{4,2,1,3,0:T(2,128)(2,1)S(1)}, u32[]{:S(2)}, u32[]{:S(2)}) collective-permute-start(bf16[1,2,2,1,512]{4,2,1,3,0:T(2,128)(2,1)S(1)} %maximum_bitcast_fusion), channel_id=1, source_target_pairs={{0,160},{32,128},{64,224},{96,192},{128,32},{160,0},{192,96},{224,... | collective-permute-start | bytes 12296 | tf_op jit(solution)/shard_map/ppermute | solution.py:24
  53.4 37.6 %collective-permute-start.5 = (bf16[1,2,2,1,512]{4,2,1,3,0:T(2,128)(2,1)S(1)}, bf16[1,2,2,1,512]{4,2,1,3,0:T(2,128)(2,1)S(1)}, u32[]{:S(2)}, u32[]{:S(2)}) collective-permute-start(bf16[1,2,2,1,512]{4,2,1,3,0:T(2,128)(2,1)S(1)} %maximum_bitcast_fusion), channel_id=1, source_target_pairs={{0,192},{32,224},{64,128},{96,160},{128,64},{160,96},{192,0},{224,... | collective-permute-start | bytes 12296 | tf_op jit(solution)/shard_map/ppermute | solution.py:24
  63.7 32.4 %collective-permute-start.6 = (bf16[1,2,2,1,512]{4,2,1,3,0:T(2,128)(2,1)S(1)}, bf16[1,2,2,1,512]{4,2,1,3,0:T(2,128)(2,1)S(1)}, u32[]{:S(2)}, u32[]{:S(2)}) collective-permute-start(bf16[1,2,2,1,512]{4,2,1,3,0:T(2,128)(2,1)S(1)} %maximum_bitcast_fusion), channel_id=1, source_target_pairs={{0,224},{32,192},{64,160},{96,128},{128,96},{160,64},{192,32},{224... | collective-permute-start | bytes 12296 | tf_op jit(solution)/shard_map/ppermute | solution.py:24
  66.5 35.9 %collective-permute-start.7 = (bf16[1,2,2,1,512]{4,2,1,3,0:T(2,128)(2,1)S(1)}, bf16[1,2,2,1,512]{4,2,1,3,0:T(2,128)(2,1)S(1)}, u32[]{:S(2)}, u32[]{:S(2)}) collective-permute-start(bf16[1,2,2,1,512]{4,2,1,3,0:T(2,128)(2,1)S(1)} %maximum_bitcast_fusion), channel_id=1, source_target_pairs={{0,256},{32,288},{64,320},{96,352},{128,384},{160,416},{192,448},{... | collective-permute-start | bytes 12296 | tf_op jit(solution)/shard_map/ppermute | solution.py:24
  80.0 28.0 %collective-permute-start.8 = (bf16[1,2,2,1,512]{4,2,1,3,0:T(2,128)(2,1)S(1)}, bf16[1,2,2,1,512]{4,2,1,3,0:T(2,128)(2,1)S(1)}, u32[]{:S(2)}, u32[]{:S(2)}) collective-permute-start(bf16[1,2,2,1,512]{4,2,1,3,0:T(2,128)(2,1)S(1)} %maximum_bitcast_fusion), channel_id=1, source_target_pairs={{0,288},{32,256},{64,352},{96,320},{128,416},{160,384},{192,480},{... | collective-permute-start | bytes 12296 | tf_op jit(solution)/shard_map/ppermute | solution.py:24
  82.9 33.9 %collective-permute-start.9 = (bf16[1,2,2,1,512]{4,2,1,3,0:T(2,128)(2,1)S(1)}, bf16[1,2,2,1,512]{4,2,1,3,0:T(2,128)(2,1)S(1)}, u32[]{:S(2)}, u32[]{:S(2)}) collective-permute-start(bf16[1,2,2,1,512]{4,2,1,3,0:T(2,128)(2,1)S(1)} %maximum_bitcast_fusion), channel_id=1, source_target_pairs={{0,320},{32,352},{64,256},{96,288},{128,448},{160,480},{192,384},{... | collective-permute-start | bytes 12296 | tf_op jit(solution)/shard_map/ppermute | solution.py:24
  91.0 28.6 %collective-permute-start.10 = (bf16[1,2,2,1,512]{4,2,1,3,0:T(2,128)(2,1)S(1)}, bf16[1,2,2,1,512]{4,2,1,3,0:T(2,128)(2,1)S(1)}, u32[]{:S(2)}, u32[]{:S(2)}) collective-permute-start(bf16[1,2,2,1,512]{4,2,1,3,0:T(2,128)(2,1)S(1)} %maximum_bitcast_fusion), channel_id=1, source_target_pairs={{0,352},{32,320},{64,288},{96,256},{128,480},{160,448},{192,416},{... | collective-permute-start | bytes 12296 | tf_op jit(solution)/shard_map/ppermute | solution.py:24
  96.1 24.5 %collective-permute-start.11 = (bf16[1,2,2,1,512]{4,2,1,3,0:T(2,128)(2,1)S(1)}, bf16[1,2,2,1,512]{4,2,1,3,0:T(2,128)(2,1)S(1)}, u32[]{:S(2)}, u32[]{:S(2)}) collective-permute-start(bf16[1,2,2,1,512]{4,2,1,3,0:T(2,128)(2,1)S(1)} %maximum_bitcast_fusion), channel_id=1, source_target_pairs={{0,384},{32,416},{64,448},{96,480},{128,256},{160,288},{192,320},{... | collective-permute-start | bytes 12296 | tf_op jit(solution)/shard_map/ppermute | solution.py:24
  102.5 19.0 %collective-permute-start.12 = (bf16[1,2,2,1,512]{4,2,1,3,0:T(2,128)(2,1)S(1)}, bf16[1,2,2,1,512]{4,2,1,3,0:T(2,128)(2,1)S(1)}, u32[]{:S(2)}, u32[]{:S(2)}) collective-permute-start(bf16[1,2,2,1,512]{4,2,1,3,0:T(2,128)(2,1)S(1)} %maximum_bitcast_fusion), channel_id=1, source_target_pairs={{0,416},{32,384},{64,480},{96,448},{128,288},{160,256},{192,352},{... | collective-permute-start | bytes 12296 | tf_op jit(solution)/shard_map/ppermute | solution.py:24
  108.0 14.4 %collective-permute-start.13 = (bf16[1,2,2,1,512]{4,2,1,3,0:T(2,128)(2,1)S(1)}, bf16[1,2,2,1,512]{4,2,1,3,0:T(2,128)(2,1)S(1)}, u32[]{:S(2)}, u32[]{:S(2)}) collective-permute-start(bf16[1,2,2,1,512]{4,2,1,3,0:T(2,128)(2,1)S(1)} %maximum_bitcast_fusion), channel_id=1, source_target_pairs={{0,448},{32,480},{64,384},{96,416},{128,320},{160,352},{192,256},{... | collective-permute-start | bytes 12296 | tf_op jit(solution)/shard_map/ppermute | solution.py:24
  116.7 6.6 %collective-permute-start.14 = (bf16[1,2,2,1,512]{4,2,1,3,0:T(2,128)(2,1)S(1)}, bf16[1,2,2,1,512]{4,2,1,3,0:T(2,128)(2,1)S(1)}, u32[]{:S(2)}, u32[]{:S(2)}) collective-permute-start(bf16[1,2,2,1,512]{4,2,1,3,0:T(2,128)(2,1)S(1)} %maximum_bitcast_fusion), channel_id=1, source_target_pairs={{0,480},{32,448},{64,416},{96,384},{128,352},{160,320},{192,288},{... | collective-permute-start | bytes 12296 | tf_op jit(solution)/shard_map/ppermute | solution.py:24
  136.6 23.3 %collective-permute-start.15 = (bf16[1,2,2,1,512]{4,2,1,3,0:T(2,128)(2,1)S(1)}, bf16[1,2,2,1,512]{4,2,1,3,0:T(2,128)(2,1)S(1)}, u32[]{:S(2)}, u32[]{:S(2)}) collective-permute-start(bf16[1,2,2,1,512]{4,2,1,3,0:T(2,128)(2,1)S(1)} %maximum_bitcast_fusion.1), channel_id=1, source_target_pairs={{0,32},{32,0},{64,96},{96,64},{128,160},{160,128},{192,224},{224,1... | collective-permute-start | bytes 12296 | tf_op jit(solution)/shard_map/ppermute | solution.py:24
  139.6 26.7 %collective-permute-start.16 = (bf16[1,2,2,1,512]{4,2,1,3,0:T(2,128)(2,1)S(1)}, bf16[1,2,2,1,512]{4,2,1,3,0:T(2,128)(2,1)S(1)}, u32[]{:S(2)}, u32[]{:S(2)}) collective-permute-start(bf16[1,2,2,1,512]{4,2,1,3,0:T(2,128)(2,1)S(1)} %maximum_bitcast_fusion.1), channel_id=1, source_target_pairs={{0,64},{32,96},{64,0},{96,32},{128,192},{160,224},{192,128},{224,1... | collective-permute-start | bytes 12296 | tf_op jit(solution)/shard_map/ppermute | solution.py:24
  145.1 27.6 %collective-permute-start.17 = (bf16[1,2,2,1,512]{4,2,1,3,0:T(2,128)(2,1)S(1)}, bf16[1,2,2,1,512]{4,2,1,3,0:T(2,128)(2,1)S(1)}, u32[]{:S(2)}, u32[]{:S(2)}) collective-permute-start(bf16[1,2,2,1,512]{4,2,1,3,0:T(2,128)(2,1)S(1)} %maximum_bitcast_fusion.1), channel_id=1, source_target_pairs={{0,96},{32,64},{64,32},{96,0},{128,224},{160,192},{192,160},{224,1... | collective-permute-start | bytes 12296 | tf_op jit(solution)/shard_map/ppermute | solution.py:24
  147.0 34.5 %collective-permute-start.18 = (bf16[1,2,2,1,512]{4,2,1,3,0:T(2,128)(2,1)S(1)}, bf16[1,2,2,1,512]{4,2,1,3,0:T(2,128)(2,1)S(1)}, u32[]{:S(2)}, u32[]{:S(2)}) collective-permute-start(bf16[1,2,2,1,512]{4,2,1,3,0:T(2,128)(2,1)S(1)} %maximum_bitcast_fusion.1), channel_id=1, source_target_pairs={{0,128},{32,160},{64,192},{96,224},{128,0},{160,32},{192,64},{224,... | collective-permute-start | bytes 12296 | tf_op jit(solution)/shard_map/ppermute | solution.py:24
  153.8 33.9 %collective-permute-start.19 = (bf16[1,2,2,1,512]{4,2,1,3,0:T(2,128)(2,1)S(1)}, bf16[1,2,2,1,512]{4,2,1,3,0:T(2,128)(2,1)S(1)}, u32[]{:S(2)}, u32[]{:S(2)}) collective-permute-start(bf16[1,2,2,1,512]{4,2,1,3,0:T(2,128)(2,1)S(1)} %maximum_bitcast_fusion.1), channel_id=1, source_target_pairs={{0,160},{32,128},{64,224},{96,192},{128,32},{160,0},{192,96},{224,... | collective-permute-start | bytes 12296 | tf_op jit(solution)/shard_map/ppermute | solution.py:24
  159.8 34.2 %collective-permute-start.20 = (bf16[1,2,2,1,512]{4,2,1,3,0:T(2,128)(2,1)S(1)}, bf16[1,2,2,1,512]{4,2,1,3,0:T(2,128)(2,1)S(1)}, u32[]{:S(2)}, u32[]{:S(2)}) collective-permute-start(bf16[1,2,2,1,512]{4,2,1,3,0:T(2,128)(2,1)S(1)} %maximum_bitcast_fusion.1), channel_id=1, source_target_pairs={{0,192},{32,224},{64,128},{96,160},{128,64},{160,96},{192,0},{224,... | collective-permute-start | bytes 12296 | tf_op jit(solution)/shard_map/ppermute | solution.py:24
  166.4 35.4 %collective-permute-start.21 = (bf16[1,2,2,1,512]{4,2,1,3,0:T(2,128)(2,1)S(1)}, bf16[1,2,2,1,512]{4,2,1,3,0:T(2,128)(2,1)S(1)}, u32[]{:S(2)}, u32[]{:S(2)}) collective-permute-start(bf16[1,2,2,1,512]{4,2,1,3,0:T(2,128)(2,1)S(1)} %maximum_bitcast_fusion.1), channel_id=1, source_target_pairs={{0,224},{32,192},{64,160},{96,128},{128,96},{160,64},{192,32},{224... | collective-permute-start | bytes 12296 | tf_op jit(solution)/shard_map/ppermute | solution.py:24
  172.7 32.9 %collective-permute-start.22 = (bf16[1,2,2,1,512]{4,2,1,3,0:T(2,128)(2,1)S(1)}, bf16[1,2,2,1,512]{4,2,1,3,0:T(2,128)(2,1)S(1)}, u32[]{:S(2)}, u32[]{:S(2)}) collective-permute-start(bf16[1,2,2,1,512]{4,2,1,3,0:T(2,128)(2,1)S(1)} %maximum_bitcast_fusion.1), channel_id=1, source_target_pairs={{0,256},{32,288},{64,320},{96,352},{128,384},{160,416},{192,448},{... | collective-permute-start | bytes 12296 | tf_op jit(solution)/shard_map/ppermute | solution.py:24
  181.4 31.5 %collective-permute-start.23 = (bf16[1,2,2,1,512]{4,2,1,3,0:T(2,128)(2,1)S(1)}, bf16[1,2,2,1,512]{4,2,1,3,0:T(2,128)(2,1)S(1)}, u32[]{:S(2)}, u32[]{:S(2)}) collective-permute-start(bf16[1,2,2,1,512]{4,2,1,3,0:T(2,128)(2,1)S(1)} %maximum_bitcast_fusion.1), channel_id=1, source_target_pairs={{0,288},{32,256},{64,352},{96,320},{128,416},{160,384},{192,480},{... | collective-permute-start | bytes 12296 | tf_op jit(solution)/shard_map/ppermute | solution.py:24
  187.7 30.7 %collective-permute-start.24 = (bf16[1,2,2,1,512]{4,2,1,3,0:T(2,128)(2,1)S(1)}, bf16[1,2,2,1,512]{4,2,1,3,0:T(2,128)(2,1)S(1)}, u32[]{:S(2)}, u32[]{:S(2)}) collective-permute-start(bf16[1,2,2,1,512]{4,2,1,3,0:T(2,128)(2,1)S(1)} %maximum_bitcast_fusion.1), channel_id=1, source_target_pairs={{0,320},{32,352},{64,256},{96,288},{128,448},{160,480},{192,384},{... | collective-permute-start | bytes 12296 | tf_op jit(solution)/shard_map/ppermute | solution.py:24
  194.0 28.5 %collective-permute-start.25 = (bf16[1,2,2,1,512]{4,2,1,3,0:T(2,128)(2,1)S(1)}, bf16[1,2,2,1,512]{4,2,1,3,0:T(2,128)(2,1)S(1)}, u32[]{:S(2)}, u32[]{:S(2)}) collective-permute-start(bf16[1,2,2,1,512]{4,2,1,3,0:T(2,128)(2,1)S(1)} %maximum_bitcast_fusion.1), channel_id=1, source_target_pairs={{0,352},{32,320},{64,288},{96,256},{128,480},{160,448},{192,416},{... | collective-permute-start | bytes 12296 | tf_op jit(solution)/shard_map/ppermute | solution.py:24
  201.8 21.6 %collective-permute-start.26 = (bf16[1,2,2,1,512]{4,2,1,3,0:T(2,128)(2,1)S(1)}, bf16[1,2,2,1,512]{4,2,1,3,0:T(2,128)(2,1)S(1)}, u32[]{:S(2)}, u32[]{:S(2)}) collective-permute-start(bf16[1,2,2,1,512]{4,2,1,3,0:T(2,128)(2,1)S(1)} %maximum_bitcast_fusion.1), channel_id=1, source_target_pairs={{0,384},{32,416},{64,448},{96,480},{128,256},{160,288},{192,320},{... | collective-permute-start | bytes 12296 | tf_op jit(solution)/shard_map/ppermute | solution.py:24
  205.6 27.3 %copy-start.2 = (bf16[1,2,512,512]{3,2,1,0:T(8,128)(2,1)S(1)}, bf16[1,2,512,512]{3,2,1,0:T(8,128)(2,1)}, u32[]{:S(2)}) copy-start(bf16[1,2,512,512]{3,2,1,0:T(8,128)(2,1)} %param.11) | copy-start | bytes 3145732
  205.6 18.8 %collective-permute-start.27 = (bf16[1,2,2,1,512]{4,2,1,3,0:T(2,128)(2,1)S(1)}, bf16[1,2,2,1,512]{4,2,1,3,0:T(2,128)(2,1)S(1)}, u32[]{:S(2)}, u32[]{:S(2)}) collective-permute-start(bf16[1,2,2,1,512]{4,2,1,3,0:T(2,128)(2,1)S(1)} %maximum_bitcast_fusion.1), channel_id=1, source_target_pairs={{0,416},{32,384},{64,480},{96,448},{128,288},{160,256},{192,352},{... | collective-permute-start | bytes 12296 | tf_op jit(solution)/shard_map/ppermute | solution.py:24
  212.9 12.4 %collective-permute-start.28 = (bf16[1,2,2,1,512]{4,2,1,3,0:T(2,128)(2,1)S(1)}, bf16[1,2,2,1,512]{4,2,1,3,0:T(2,128)(2,1)S(1)}, u32[]{:S(2)}, u32[]{:S(2)}) collective-permute-start(bf16[1,2,2,1,512]{4,2,1,3,0:T(2,128)(2,1)S(1)} %maximum_bitcast_fusion.1), channel_id=1, source_target_pairs={{0,448},{32,480},{64,384},{96,416},{128,320},{160,352},{192,256},{... | collective-permute-start | bytes 12296 | tf_op jit(solution)/shard_map/ppermute | solution.py:24
  218.3 7.9 %collective-permute-start.29 = (bf16[1,2,2,1,512]{4,2,1,3,0:T(2,128)(2,1)S(1)}, bf16[1,2,2,1,512]{4,2,1,3,0:T(2,128)(2,1)S(1)}, u32[]{:S(2)}, u32[]{:S(2)}) collective-permute-start(bf16[1,2,2,1,512]{4,2,1,3,0:T(2,128)(2,1)S(1)} %maximum_bitcast_fusion.1), channel_id=1, source_target_pairs={{0,480},{32,448},{64,416},{96,384},{128,352},{160,320},{192,288},{... | collective-permute-start | bytes 12296 | tf_op jit(solution)/shard_map/ppermute | solution.py:24
